TPU v7x, 512 devices: a whole 4x8x8 slice. The times are simulated.
512 devices in a mesh: segment: 4 (over x), shard: 128 (over z, y, core).
Axes of the slice: x: 4, y: 8, z: 8, core: 2. Of those that a mesh axis runs over, the one named last changes fastest.
Arguments:
- proposal_attributes: bfloat16 [2, 65536, 1024], P(None, 'shard'), may hold values from -6 to 6
- keeper_ordering_vectors: bfloat16 [2, 16384, 4096], P(None, 'shard'), may hold values from -6 to 6
- keeper_positions: int32 [2, 16384], P(None, 'shard'), may hold values from 0 to 511
- alive_tallies: int32 [2, 128], P(None, 'shard'), may hold values from 256 to 512
- holder_shards: int32 [2, 16384, 1], P(None, 'shard'), may hold values from 0 to 127; in each aligned block of 128 rows (0 to 127, 128 to 255, ..., all dimensions but the last counted through in order) at most 2 rows name the same one
- holder_attribute_factor: bfloat16 [128, 4096], P('shard'), may hold values from 0.099609375 to 1.8984375
- early_inner_matrix: bfloat16 [1024, 1024], replicated, may hold values from -0.1875 to 0.1875
- early_inner_offset: float32 [1024], replicated, may hold values from -3 to 3
- early_grading_vector: bfloat16 [1024], replicated, may hold values from -0.1875 to 0.1875
- block_lowering_matrices: bfloat16 [3, 4096, 128], P(None, 'shard'), may hold values from -0.09375 to 0.09375
- block_raising_flipped: bfloat16 [3, 4096, 128], P(None, 'shard'), may hold values from -0.5 to 0.5
- block_result_offsets: float32 [3, 4096], replicated, may hold values from -3 to 3
- block_grading_vectors: float32 [3, 4096], replicated, may hold values from -0.09375 to 0.09375
Outputs:
- exits: float32 [4, 2, 32768], P('segment', None, 'shard')
Inputs may be any that keep to these rules, and one draw needn't show every extreme that they name: `holder_shards`: in every round at most 2 entries of one block of 128 go to one owner. `keeper_positions`: entries at or above the block's count in alive_tallies are padding.
All inputs are finite; a program needn't handle non-finite values.
Results may differ from a plain program's by a relative error of at most 0.02.
Values may be sent and summed in bfloat16 or wider, within the bound.
A program may use at most 64 MiB of HBM per device.

v0:
```python
import jax
import jax.numpy as jnp
from jax import lax
from jax.sharding import PartitionSpec as P

F32 = jnp.float32
BF16 = jnp.bfloat16
HIGH = lax.Precision.HIGHEST
LANES = 128


def fdot(a, b, precision=None):
    return jnp.dot(a, b, preferred_element_type=F32, precision=precision)


def gather_blocks(block):
    return lax.all_gather(block, "shard", axis=0, tiled=False)


def sum_segments(value):
    return lax.psum(value, "segment")


def local(
    proposal_attributes,
    keeper_ordering_vectors,
    keeper_positions,
    alive_tallies,
    holder_shards,
    holder_attribute_factor,
    early_inner_matrix,
    early_inner_offset,
    early_grading_vector,
    block_lowering_matrices,
    block_raising_flipped,
    block_result_offsets,
    block_grading_vectors,
):
    segment_id = lax.axis_index("segment")
    segment_count = lax.axis_size("segment")
    shard_count = lax.axis_size("shard")
    rounds, entries, width = keeper_ordering_vectors.shape
    candidates = proposal_attributes.shape[1]
    low_rank = block_lowering_matrices.shape[2]
    cap_slots = max(2, 2 * entries // shard_count)
    rows = rounds * entries
    own_features = width // shard_count
    piece = own_features // segment_count
    part_width = width // segment_count
    span = segment_count * LANES
    spans = width // span
    at = lax.broadcasted_iota(jnp.int32, (span, LANES), 0)
    to = lax.broadcasted_iota(jnp.int32, (span, LANES), 1)
    chosen = (at // own_features == to // piece) & (
        at % own_features == segment_id * piece + to % piece
    )
    pick = chosen.astype(BF16)
    pick32 = chosen.astype(F32)

    def part_of(values):
        return [fdot(values[:, g * span : (g + 1) * span], pick) for g in range(spans)]

    def part_of32(values):
        return jnp.concatenate(
            [fdot(values[:, g * span : (g + 1) * span], pick32, HIGH) for g in range(spans)], 1
        )

    own_gain = jnp.concatenate(part_of(holder_attribute_factor), 0).astype(BF16)
    own_lower = lax.dynamic_slice_in_dim(block_lowering_matrices, segment_id * piece, piece, 1)
    own_raise = lax.dynamic_slice_in_dim(block_raising_flipped, segment_id * piece, piece, 1)
    block = jnp.concatenate(
        [own_lower.reshape(3 * piece, low_rank), own_raise.reshape(3 * piece, low_rank), own_gain],
        0,
    )
    blocks = gather_blocks(block)

    def matrix(k):
        return blocks[:, k * piece : (k + 1) * piece].reshape(part_width, low_rank)

    hidden = jax.nn.relu(
        fdot(proposal_attributes.reshape(rounds * candidates, -1), early_inner_matrix)
        + early_inner_offset
    ).astype(BF16)
    scores = fdot(hidden, early_grading_vector).reshape(rounds, candidates)
    ids = jnp.arange(candidates, dtype=jnp.int32)
    looked_up = jnp.sum(
        jnp.where(keeper_positions[:, :, None] == ids, scores[:, None, :], 0.0), axis=2
    )
    keep = (keeper_positions < alive_tallies).astype(F32)
    gate = jax.nn.sigmoid(looked_up) * keep
    owner = holder_shards[:, :, 0]
    order = jnp.arange(entries, dtype=jnp.int32)
    same = (owner[:, :, None] == owner[:, None, :]) & (order[None, :] < order[:, None])
    within = jnp.sum(same.astype(jnp.int32), axis=2)
    target = owner * cap_slots + within
    slots = jnp.arange(shard_count * cap_slots, dtype=jnp.int32)
    placed = slots[None, :, None] == target[:, None, :]
    gate_col = gate.reshape(rows, 1)
    keep_col = keep.reshape(rows, 1)
    own_rows = jnp.concatenate(part_of(keeper_ordering_vectors.reshape(rows, width)), 1)
    h0 = (own_rows * gate_col).astype(BF16)
    owner_hot = (
        owner.reshape(rows, 1) == jnp.arange(shard_count, dtype=jnp.int32)[None, :]
    ).astype(BF16)
    gains = jnp.concatenate(
        [fdot(owner_hot, blocks[:, 6 * piece + g]) for g in range(part_width // LANES)], 1
    )
    x = (h0.astype(F32) * gains).astype(BF16)
    biases = part_of32(block_result_offsets)
    heads = part_of32(block_grading_vectors)
    lower1, lower2, lower3, raise1, raise2, raise3 = [matrix(k) for k in range(6)]
    between = lax.dot_general(raise2, lower3, (((0,), (0,)), ((), ())), preferred_element_type=F32)
    raised = lax.dot_general(
        heads[1:3], raise2.astype(F32), (((1,), (0,)), ((), ())), precision=HIGH
    )
    raised3 = lax.dot_general(
        heads[2:3], raise3.astype(F32), (((1,), (0,)), ((), ())), precision=HIGH
    )
    lowered_bias = lax.dot_general(
        biases[1:2], lower3.astype(F32), (((1,), (0,)), ((), ())), precision=HIGH
    )
    consts = jnp.stack(
        [
            jnp.sum(biases[1] * heads[1]),
            jnp.sum(biases[1] * heads[2]),
            jnp.sum(biases[2] * heads[2]),
        ]
    )
    consts = jnp.pad(consts, (0, low_rank - 3))[None]
    first = jnp.concatenate([fdot(x, lower1), between, raised, raised3, lowered_bias, consts], 0)
    first = sum_segments(jnp.pad(first, ((0, 3), (0, 0))))
    act1 = first[:rows].astype(BF16)
    lifted = (
        lax.dot_general(act1, raise1, (((1,), (1,)), ((), ())), preferred_element_type=F32)
        + biases[0]
    )
    x32 = x.astype(F32)
    out1 = (x32 + x32 * lifted) * keep_col
    h1 = out1.astype(BF16)
    h1_32 = h1.astype(F32)
    graded = jnp.stack(
        [
            jnp.sum(out1 * heads[0], axis=1),
            jnp.sum(h1_32 * heads[1], axis=1),
            jnp.sum(h1_32 * heads[2], axis=1),
        ]
    ).reshape(-1, low_rank)
    second = jnp.concatenate([fdot(h1, lower2), fdot(h1, lower3), graded], 0)
    second = sum_segments(jnp.pad(second, ((0, -second.shape[0] % 8), (0, 0))))
    between = first[rows : rows + low_rank]
    vectors = first[rows + low_rank : rows + low_rank + 5]
    graded = second[2 * rows : 2 * rows + 3 * rows // low_rank].reshape(3, rows)
    keep_row = keep.reshape(rows)
    act2 = jax.nn.relu(second[:rows]).astype(BF16).astype(F32)
    graded2 = graded[1] + jnp.sum(act2 * vectors[0], axis=1) + vectors[4, 0]
    inner3 = (second[rows : 2 * rows] + fdot(act2, between, HIGH) + vectors[3]) * keep_col
    act3 = jax.nn.relu(inner3).astype(BF16).astype(F32)
    graded3 = (
        (graded[2] + jnp.sum(act2 * vectors[1], axis=1) + vectors[4, 1]) * keep_row
        + jnp.sum(act3 * vectors[2], axis=1)
        + vectors[4, 2]
    )
    section = jnp.stack([gate.reshape(rows), graded[0], graded2 * keep_row, graded3 * keep_row])
    values = lax.dynamic_index_in_dim(section, segment_id, 0, keepdims=False)
    values = values.reshape(rounds, 1, entries)
    sent = jnp.sum(jnp.where(placed, values, 0.0), axis=2)
    outgoing = sent.reshape(rounds, shard_count, cap_slots).transpose(1, 0, 2)
    outgoing = outgoing.reshape(shard_count, rounds * cap_slots)
    arrived = lax.all_to_all(outgoing, "shard", split_axis=0, concat_axis=0, tiled=True)
    arrived = arrived.reshape(shard_count, rounds, cap_slots).transpose(1, 0, 2)
    arrived = arrived.reshape(rounds, shard_count * cap_slots)
    return jnp.where(segment_id == 0, sent, arrived)[None]


def solution(mesh):
    placed = (
        P(None, "shard", None),
        P(None, "shard", None),
        P(None, "shard"),
        P(None, "shard"),
        P(None, "shard", None),
        P("shard", None),
        P(),
        P(),
        P(),
        P(None, "shard", None),
        P(None, "shard", None),
        P(),
        P(),
    )
    return jax.shard_map(
        local, mesh=mesh, in_specs=placed, out_specs=P("segment", None, "shard"), check_vma=False
    )
```

profile of v0, /device:TPU:1, one launch (start us, length us, event | category | flops | bytes accessed | tf_op | source)
XLA Modules:
  0.0 260.8 jit_solution(11579320052899533610)
XLA Ops:
  14.6 1.8 concatenate.25
  18.0 0.9 fusion.27
  18.9 0.9 fusion.26
  19.8 0.9 fusion.25
  20.7 0.9 fusion.24
  21.6 0.9 fusion.23
  26.0 0.9 fusion.34
  26.9 0.9 fusion.33
  29.6 4.4 %fusion = f32[1,1024]{1,0:T(1,128)S(1)} fusion(bf16[1024,1]{0,1:T(2,128)(2,1)S(1)} %reshape.249, f32[1024]{0:T(1024)} %param.20, bf16[1024,1024]{1,0:T(8,128)(2,1)S(1)} %bitcast.325, bf16[1024,1024]{1,0:T(8,128)(2,1)} %param.19), kind=kOutput, calls=%fused_computation.1 | convolution fusion | flops 2152726528 | bytes 4204544 | tf_op jit(solution)/shard_map/dot_general | solution.py:13
  34.2 1.0 fusion.30
  36.8 2.0 fusion.155
  39.2 1.8 fusion.13
  41.0 1.8 fusion.12
  42.9 1.8 fusion.11
  44.7 1.8 fusion.10
  47.4 0.9 fusion.8
  49.2 0.9 fusion.6
  50.1 55.1 %all-gather.3.cloned.1.call-done = bf16[7168,128]{1,0:T(8,128)(2,1)} async-done(((bf16[56,128]{1,0:T(8,128)(2,1)}), bf16[7168,128]{1,0:T(8,128)(2,1)}) %all-gather.3.cloned.1.call-update) | async-done | bytes 1835024 | tf_op jit(solution)/shard_map/all_gather | solution.py:17
  105.2 2.9 %fusion.164 = (bf16[128,1,128]{2,1,0:T(2,128)(2,1)S(1)}, bf16[128,1,128]{2,1,0:T(2,128)(2,1)S(1)}, bf16[128,1,128]{2,1,0:T(2,128)(2,1)S(1)}, bf16[128,1,128]{2,1...) fusion(bf16[128,56,128]{2,1,0:T(8,128)(2,1)} %bitcast.326), kind=kLoop, calls=%fused_computation.267 | loop fusion | bytes 524288 | tf_op jit(solution)/shard_map/slice | solution.py:106
  108.2 1.1 fusion.163
  112.1 1.4 multiply_convert_fusion
  114.9 46.5 %all-reduce.6.cloned.1.call-done = f32[392,128]{1,0:T(8,128)} async-done(((f32[392,128]{1,0:T(8,128)}), f32[392,128]{1,0:T(8,128)}) %all-reduce.6.cloned.1.call-update) | async-done | bytes 200720 | tf_op jit(solution)/shard_map/psum | solution.py:21
  161.4 1.7 fusion.53
  163.1 1.3 fusion.63
  164.4 1.3 fusion.76
  166.4 1.4 fusion.166
  168.7 50.7 %all-reduce.8.cloned.1.call-done = f32[520,128]{1,0:T(8,128)} async-done(((f32[520,128]{1,0:T(8,128)}), f32[520,128]{1,0:T(8,128)}) %all-reduce.8.cloned.1.call-update) | async-done | bytes 266256 | tf_op jit(solution)/shard_map/psum | solution.py:21
  220.2 1.3 fusion.20
  221.5 1.1 fusion.83
  222.5 1.9 add_multiply_fusion.1
  225.6 16.3 %all-to-all-start = ((f32[128,1,4]{2,1,0:T(1,128)}), f32[128,1,4]{2,1,0:T(1,128)S(1)}, u32[]{:S(2)}, u32[]{:S(2)}) async-start(f32[128,1,4]{2,1,0:T(1,128)} %copy.50), calls=%async_computation | async-start | bytes 131072 | tf_op jit(solution)/shard_map/all_to_all | solution.py:169
  241.9 11.4 %all-to-all-done = f32[128,1,4]{2,1,0:T(1,128)S(1)} async-done(((f32[128,1,4]{2,1,0:T(1,128)}), f32[128,1,4]{2,1,0:T(1,128)S(1)}, u32[]{:S(2)}, u32[]{:S(2)}) %all-to-all-start) | async-done | bytes 2080 | tf_op jit(solution)/shard_map/all_to_all | solution.py:169
  (85 shorter events, 27.5 us)
Async XLA Ops:
  6.5 23.1 %copy-start = (bf16[2,512,1024]{2,1,0:T(8,128)(2,1)S(1)}, bf16[2,512,1024]{2,1,0:T(8,128)(2,1)}, u32[]{:S(2)}) copy-start(bf16[2,512,1024]{2,1,0:T(8,128)(2,1)} %param.13) | copy-start | bytes 6291460
  6.5 98.7 %all-gather.3.cloned.1.call-start = ((), (), s32[]{:S(2)}) async-start(), calls=%async_computation.3 | async-start | bytes 1849344 | tf_op jit(solution)/shard_map/all_gather | solution.py:17
  16.4 144.9 %all-reduce.6.cloned.1.call-start = ((), (), s32[]{:S(2)}) async-start(), calls=%async_computation.1 | async-start | bytes 401408 | tf_op jit(solution)/shard_map/psum | solution.py:21
  29.6 4.4 %copy-start.3 = (s32[2,128]{1,0:T(2,128)S(1)}, s32[2,128]{1,0:T(2,128)}, u32[]{:S(2)}) copy-start(s32[2,128]{1,0:T(2,128)} %param.15) | copy-start | bytes 3076
  29.6 4.4 %copy-start.4 = (s32[2,1]{0,1:T(1,128)S(1)}, s32[2,1]{0,1:T(1,128)}, u32[]{:S(2)}) copy-start(s32[2,1]{0,1:T(1,128)} %param.16) | copy-start | bytes 28
  29.6 9.2 %copy-start.2 = (s32[2,128,1]{1,2,0:T(1,128)S(1)}, s32[2,128,1]{1,2,0:T(1,128)}, u32[]{:S(2)}) copy-start(s32[2,128,1]{1,2,0:T(1,128)} %param.17) | copy-start | bytes 3076
  34.1 12.4 %copy-start.5 = (bf16[2,128,4096]{2,1,0:T(8,128)(2,1)S(1)}, bf16[2,128,4096]{2,1,0:T(8,128)(2,1)}, u32[]{:S(2)}) copy-start(bf16[2,128,4096]{2,1,0:T(8,128)(2,1)} %param.14) | copy-start | bytes 6291460
  105.2 4.0 %copy-start.1 = (bf16[7168,128]{1,0:T(8,128)(2,1)S(1)}, bf16[7168,128]{1,0:T(8,128)(2,1)}, u32[]{:S(2)}) copy-start(bf16[7168,128]{1,0:T(8,128)(2,1)} %all-gather.3.cloned.1.call-done) | copy-start | bytes 5505028
  114.9 104.5 %all-reduce.8.cloned.1.call-start = ((), (), s32[]{:S(2)}) async-start(), calls=%async_computation.2 | async-start | bytes 532480 | tf_op jit(solution)/shard_map/psum | solution.py:21
  225.6 27.7 %all-to-all-start = ((f32[128,1,4]{2,1,0:T(1,128)}), f32[128,1,4]{2,1,0:T(1,128)S(1)}, u32[]{:S(2)}, u32[]{:S(2)}) async-start(f32[128,1,4]{2,1,0:T(1,128)} %copy.50), calls=%async_computation | async-start | bytes 131072 | tf_op jit(solution)/shard_map/all_to_all | solution.py:169
Sparse Core Ops, SparseCore 0:
  16.6 88.6 all-gather.2
  115.0 46.3 all-reduce.5
  166.5 52.7 all-reduce.7
where the time goes:
time: 262 us; the launch traced here: 261 us
  waiting for transfers between devices  164 us (63%)
  matrix products  45.1 us (17%)
  starting transfers between devices  16.4 us (6%)
  between operations  13.4 us (5%)
  local copies, waits for them, and re-layouts  12.4 us (5%)
  other arithmetic  9.7 us (4%)
    psum x2, waiting for transfers between devices, sum_segments(): return lax.psum(value, 'segment')  97.2 us
    all_gather x1, waiting for transfers between devices, gather_blocks(): return lax.all_gather(block, 'shard', axis=0, tiled=False)  55.1 us
    dot_general x45, matrix products, fdot(): return jnp.dot(a, b, preferred_element_type=F32, precision=precision)  42.6 us
    all_to_all x1, starting transfers between devices, local(): lax.all_to_all(outgoing, 'shard', split_axis=0, concat_axis=0, tiled=True)  16.3 us
    all_to_all x1, waiting for transfers between devices, local(): lax.all_to_all(outgoing, 'shard', split_axis=0, concat_axis=0, tiled=True)  11.4 us
  transfers between devices with their start and end apart: 4, of which 4 were waited for; matrix products, arithmetic and copies ran while one was open for 14% of the time, Pallas kernels for 0%

commit v1 on v0

--- a/solution.py
+++ b/solution.py
@@ -2,6 +2,7 @@
 import jax.numpy as jnp
 from jax import lax
 from jax.sharding import PartitionSpec as P
+from jax.lax import all_gather
 
 F32 = jnp.float32
 BF16 = jnp.bfloat16
@@ -18,7 +19,7 @@
 
 
 def sum_segments(value):
-    return lax.psum(value, "segment")
+    return all_gather(value, "segment").sum(axis=0)
 
 
 def local(

time: 262 us -> 201 us (0.77)
  waiting for transfers between devices: 164 us -> 91.5 us
  blocking collectives: 0 us -> 12 us
    psum x2 -> x0, waiting for transfers between devices: 97.2 us -> none  [sum_segments(): return lax.psum(value, 'segment')]
    all_gather x0 -> x1, waiting for transfers between devices: none -> 24.7 us  [sum_segments(): return all_gather(value, 'segment').sum(axis=0)]
    all_gather x0 -> x1, blocking collectives: none -> 12 us  [sum_segments(): return all_gather(value, 'segment').sum(axis=0)]
  transfers between devices with their start and end apart: 4 -> 3, of which waited for: 4 -> 3; matrix products, arithmetic and copies ran while one was open for 14% -> 18% of each run, Pallas kernels for 0% -> 0%
where the time goes in v1:
time: 201 us; the launch traced here: 199 us
  waiting for transfers between devices  91.5 us (46%)
  matrix products  45 us (22%)
  starting transfers between devices  15.2 us (8%)
  between operations  13.7 us (7%)
  blocking collectives  12 us (6%)
  local copies, waits for them, and re-layouts  11.1 us (6%)
  other arithmetic  10.8 us (5%)
    all_gather x1, waiting for transfers between devices, gather_blocks(): return lax.all_gather(block, 'shard', axis=0, tiled=False)  55.3 us
    dot_general x45, matrix products, fdot(): return jnp.dot(a, b, preferred_element_type=F32, precision=precision)  42.4 us
    all_gather x1, waiting for transfers between devices, sum_segments(): return all_gather(value, 'segment').sum(axis=0)  24.7 us
    all_to_all x1, starting transfers between devices, local(): lax.all_to_all(outgoing, 'shard', split_axis=0, concat_axis=0, tiled=True)  15.2 us
    all_gather x1, blocking collectives, sum_segments(): return all_gather(value, 'segment').sum(axis=0)  12 us
    all_to_all x1, waiting for transfers between devices, local(): lax.all_to_all(outgoing, 'shard', split_axis=0, concat_axis=0, tiled=True)  11.4 us
  transfers between devices with their start and end apart: 3, of which 3 were waited for; matrix products, arithmetic and copies ran while one was open for 18% of the time, Pallas kernels for 0%

profile of v1, /device:TPU:1, one launch (start us, length us, event | category | flops | bytes accessed | tf_op | source)
XLA Modules:
  0.0 199.4 jit_solution(2755291711203793521)
XLA Ops:
  14.6 1.8 concatenate.25
  18.0 0.9 fusion.27
  18.9 0.9 fusion.26
  20.7 0.9 fusion.24
  21.6 0.9 fusion.23
  26.0 0.9 fusion.34
  26.9 0.9 fusion.33
  28.7 4.4 %fusion = f32[1,1024]{1,0:T(1,128)S(1)} fusion(bf16[1024,1]{0,1:T(2,128)(2,1)S(1)} %reshape.251, f32[1024]{0:T(1024)} %param.20, bf16[1024,1024]{1,0:T(8,128)(2,1)S(1)} %bitcast.327, bf16[1024,1024]{1,0:T(8,128)(2,1)} %param.19), kind=kOutput, calls=%fused_computation.1 | convolution fusion | flops 2152726528 | bytes 4204544 | tf_op jit(solution)/shard_map/dot_general | solution.py:14
  33.1 0.9 fusion.31
  34.0 1.0 fusion.30
  36.7 2.0 fusion.154
  39.0 1.8 fusion.13
  40.8 1.8 fusion.12
  42.6 1.8 fusion.11
  44.5 1.8 fusion.10
  47.2 0.9 fusion.8
  49.0 0.9 fusion.6
  49.9 55.3 %all-gather.6.cloned.1.call-done = bf16[7168,128]{1,0:T(8,128)(2,1)} async-done(((bf16[56,128]{1,0:T(8,128)(2,1)}), bf16[7168,128]{1,0:T(8,128)(2,1)}) %all-gather.6.cloned.1.call-update) | async-done | bytes 1835024 | tf_op jit(solution)/shard_map/all_gather | solution.py:18
  105.2 2.9 %fusion.162 = (bf16[128,1,128]{2,1,0:T(2,128)(2,1)S(1)}, bf16[128,1,128]{2,1,0:T(2,128)(2,1)S(1)}, bf16[128,1,128]{2,1,0:T(2,128)(2,1)S(1)}, bf16[128,1,128]{2,1...) fusion(bf16[128,56,128]{2,1,0:T(8,128)(2,1)} %bitcast.328), kind=kLoop, calls=%fused_computation.266 | loop fusion | bytes 524288 | tf_op jit(solution)/shard_map/slice | solution.py:107
  108.2 1.1 fusion.161
  112.0 1.4 multiply_convert_fusion
  114.1 12.0 %all-gather.1 = f32[1568,128]{1,0:T(8,128)S(1)} all-gather(f32[392,128]{1,0:T(8,128)S(1)} %pad.13), channel_id=3, replica_groups=mesh['segment'=4,'shard'=128] {'segment'}, dimensions={0}, use_global_device_ids=true | all-gather | bytes 1003520 | tf_op jit(solution)/shard_map/all_gather | solution.py:22
  126.8 1.7 fusion.53
  128.5 1.3 fusion.63
  129.8 1.3 fusion.76
  132.1 1.4 fusion.164
  134.3 24.7 %all-gather.8.cloned.1.call-done = f32[2080,128]{1,0:T(8,128)} async-done(((f32[520,128]{1,0:T(8,128)}), f32[2080,128]{1,0:T(8,128)}) %all-gather.8.cloned.1.call-update) | async-done | bytes 1064976 | tf_op jit(solution)/shard_map/all_gather | solution.py:22
  159.1 1.3 reduce_sum.143
  160.8 1.1 fusion.20
  161.9 1.9 add_multiply_fusion.1
  165.0 15.2 %all-to-all-start = ((f32[128,1,4]{2,1,0:T(1,128)}), f32[128,1,4]{2,1,0:T(1,128)S(1)}, u32[]{:S(2)}, u32[]{:S(2)}) async-start(f32[128,1,4]{2,1,0:T(1,128)} %copy.55), calls=%async_computation | async-start | bytes 131072 | tf_op jit(solution)/shard_map/all_to_all | solution.py:170
  180.2 11.4 %all-to-all-done = f32[128,1,4]{2,1,0:T(1,128)S(1)} async-done(((f32[128,1,4]{2,1,0:T(1,128)}), f32[128,1,4]{2,1,0:T(1,128)S(1)}, u32[]{:S(2)}, u32[]{:S(2)}) %all-to-all-start) | async-done | bytes 2080 | tf_op jit(solution)/shard_map/all_to_all | solution.py:170
  (89 shorter events, 27.0 us)
Async XLA Ops:
  6.5 22.2 %copy-start = (bf16[2,512,1024]{2,1,0:T(8,128)(2,1)S(1)}, bf16[2,512,1024]{2,1,0:T(8,128)(2,1)}, u32[]{:S(2)}) copy-start(bf16[2,512,1024]{2,1,0:T(8,128)(2,1)} %param.13) | copy-start | bytes 6291460
  6.5 98.7 %all-gather.6.cloned.1.call-start = ((), (), s32[]{:S(2)}) async-start(), calls=%async_computation.1 | async-start | bytes 1849344 | tf_op jit(solution)/shard_map/all_gather | solution.py:18
  16.4 142.6 %all-gather.8.cloned.1.call-start = ((), (), s32[]{:S(2)}) async-start(), calls=%async_computation.2 | async-start | bytes 1331200 | tf_op jit(solution)/shard_map/all_gather | solution.py:22
  28.7 10.0 %copy-start.3 = (s32[2,128]{1,0:T(2,128)S(1)}, s32[2,128]{1,0:T(2,128)}, u32[]{:S(2)}) copy-start(s32[2,128]{1,0:T(2,128)} %param.15) | copy-start | bytes 3076
  28.7 10.2 %copy-start.4 = (s32[2,1]{0,1:T(1,128)S(1)}, s32[2,1]{0,1:T(1,128)}, u32[]{:S(2)}) copy-start(s32[2,1]{0,1:T(1,128)} %param.16) | copy-start | bytes 28
  34.0 12.3 %copy-start.5 = (bf16[2,128,4096]{2,1,0:T(8,128)(2,1)S(1)}, bf16[2,128,4096]{2,1,0:T(8,128)(2,1)}, u32[]{:S(2)}) copy-start(bf16[2,128,4096]{2,1,0:T(8,128)(2,1)} %param.14) | copy-start | bytes 6291460
  48.1 61.8 %copy-start.2 = (s32[2,128,1]{1,2,0:T(1,128)S(1)}, s32[2,128,1]{1,2,0:T(1,128)}, u32[]{:S(2)}) copy-start(s32[2,128,1]{1,2,0:T(1,128)} %param.17) | copy-start | bytes 3076
  105.2 4.0 %copy-start.1 = (bf16[7168,128]{1,0:T(8,128)(2,1)S(1)}, bf16[7168,128]{1,0:T(8,128)(2,1)}, u32[]{:S(2)}) copy-start(bf16[7168,128]{1,0:T(8,128)(2,1)} %all-gather.6.cloned.1.call-done) | copy-start | bytes 5505028
  165.0 26.6 %all-to-all-start = ((f32[128,1,4]{2,1,0:T(1,128)}), f32[128,1,4]{2,1,0:T(1,128)S(1)}, u32[]{:S(2)}, u32[]{:S(2)}) async-start(f32[128,1,4]{2,1,0:T(1,128)} %copy.55), calls=%async_computation | async-start | bytes 131072 | tf_op jit(solution)/shard_map/all_to_all | solution.py:170
Sparse Core Ops, SparseCore 0:
  16.6 88.6 all-gather.5
  132.0 27.0 all-gather.7
